TPU v7x, 32 devices: a whole 2x2x4 slice. The times are simulated.
32 devices in a mesh: band: 4 (over y, x), query: 8 (over z, core).
Axes of the slice: x: 2, y: 2, z: 4, core: 2. Of those that a mesh axis runs over, the one named last changes fastest.
Arguments:
- spectra: bfloat16 [192, 20480], P('band'), may hold values from 0 to 3
- theo: bfloat16 [8, 8, 20480], P('query', 'band'), may hold values from -0.0390625 to 0.0390625
- offsets: int32 [16], replicated, may hold values from -128 to 128
- win_lo: int32 [192], P('band'), may hold values from 0 to 32
- win_len: int32 [192], P('band'), may hold values from 1 to 32
Outputs:
- best: float32 [192, 16], P(('band', 'query'))
- average: float32 [192, 16], P(('band', 'query'))
Inputs may be any that keep to these rules, and one draw needn't show every extreme that they name: win_lo + win_len never exceeds 64.
All inputs are finite; a program needn't handle non-finite values.
Results may differ from a plain program's by a relative error of at most 0.003.
Values may be sent and summed in bfloat16 or wider, within the bound.
A program may use at most 128 MiB of HBM per device.

v0:
```python
import jax
import jax.numpy as jnp
from jax import lax
from jax.sharding import PartitionSpec as P

BG_HALF = 75
SHIFT_MAX = 128


def box_table():
    source = lax.broadcasted_iota(jnp.int32, (384, 128), 0)
    target = lax.broadcasted_iota(jnp.int32, (384, 128), 1)
    offset_gap = source - 128 - target
    inside = (jnp.abs(offset_gap) <= BG_HALF) & (offset_gap != 0)
    return inside.astype(jnp.bfloat16)


def correct(intensity):
    row_count, bin_count = intensity.shape
    block_count = bin_count // 128
    blocks = intensity.reshape(row_count, block_count, 128)
    zero_block = jnp.zeros((row_count, 1, 128), intensity.dtype)
    previous = jnp.concatenate([zero_block, blocks[:, :-1]], axis=1)
    following = jnp.concatenate([blocks[:, 1:], zero_block], axis=1)
    stacked = jnp.concatenate([previous, blocks, following], axis=2)
    window_sum = jnp.einsum("rbj,ji->rbi", stacked, box_table(), preferred_element_type=jnp.float32)
    result = blocks.astype(jnp.float32) - window_sum / (2.0 * BG_HALF)
    return result.astype(jnp.bfloat16).reshape(row_count, bin_count)


def shifted_copies(peptides, offsets):
    bin_count = peptides.shape[1]
    padded = jnp.pad(peptides, ((0, 0), (SHIFT_MAX, SHIFT_MAX)))

    def take_shift(offset):
        return lax.dynamic_slice_in_dim(padded, SHIFT_MAX - offset, bin_count, 1)

    copies = jax.vmap(take_shift, out_axes=1)(offsets)
    return copies.reshape(-1, bin_count)


def local(spectra, theo, offsets, win_lo, win_len):
    query_count = lax.axis_size("query")
    spectra_rows = spectra.shape[0]
    own_rows = spectra_rows // query_count
    own_start = lax.axis_index("query") * own_rows
    corrected = correct(spectra)
    shift_count = offsets.shape[0]
    group_size = theo.shape[1] * lax.axis_size("band")
    piece = lax.all_gather(theo, "band", axis=1, tiled=True)
    piece_rows = piece.shape[1]
    copies = shifted_copies(piece[0], offsets)
    partial_scores = jnp.einsum("mb,sb->ms", copies, corrected, preferred_element_type=jnp.float32)
    scores = partial_scores.reshape(1, piece_rows, shift_count * spectra_rows)
    score_table = scores.reshape(group_size, shift_count, query_count, own_rows)
    low_own = lax.dynamic_slice_in_dim(win_lo, own_start, own_rows, 0)
    length_own = lax.dynamic_slice_in_dim(win_len, own_start, own_rows, 0)
    gathered = lax.all_to_all(score_table, "query", split_axis=2, concat_axis=0, tiled=True)
    total_peptides = gathered.shape[0]
    owned_scores = gathered.reshape(total_peptides, shift_count, own_rows)
    peptide_index = lax.broadcasted_iota(jnp.int32, (total_peptides, own_rows), 0)
    inside = (peptide_index >= low_own[None, :]) & (peptide_index < (low_own + length_own)[None, :])
    best_score = jnp.max(jnp.where(inside[:, None, :], owned_scores, -jnp.inf), axis=0).T
    totals = jnp.sum(jnp.where(inside[:, None, :], owned_scores, 0.0), axis=0).T
    average = totals / length_own[:, None].astype(jnp.float32)
    return (best_score, average)


def solution(mesh):
    placed = (P("band", None), P("query", "band", None), P(), P("band"), P("band"))
    return jax.shard_map(
        local,
        mesh=mesh,
        in_specs=placed,
        out_specs=(P(("band", "query"), None), P(("band", "query"), None)),
        check_vma=False,
    )
```

profile of v0, /device:TPU:0, one launch (start us, length us, event | category | flops | bytes accessed | tf_op | source)
XLA Modules:
  0.0 84.9 jit_solution(6701654885838280901)
XLA Ops:
  0.7 1.2 %copy.17 = bf16[1,2,20480]{2,0,1:T(2,128)(2,1)S(1)} copy(bf16[1,2,20480]{2,1,0:T(2,128)(2,1)} %param.6) | data formatting | bytes 163840 | tf_op args[1]
  1.8 12.0 %all_gather.3 = bf16[1,8,20480]{2,0,1:T(2,128)(2,1)S(1)} all-gather(bf16[1,2,20480]{2,0,1:T(2,128)(2,1)S(1)} %copy.17), channel_id=1, replica_groups=mesh['band'=4,'query'=8] {'band'}, dimensions={1}, use_global_device_ids=true | all-gather | bytes 409600 | tf_op jit(solution)/shard_map/all_gather | solution.py:50
  13.8 0.4 copy.28
  14.2 0.7 fusion.29
  14.9 34.0 %while.1 = (s32[]{:T(128)}, bf16[8,20736]{1,0:T(8,128)(2,1)S(1)}, s32[16,2]{0,1:T(2,128)S(1)}, bf16[16,8,20480]{2,1,0:T(8,128)(2,1)}, s32[]{:T(128)}) while((s32[]{:T(128)}, bf16[8,20736]{1,0:T(8,128)(2,1)S(1)}, s32[16,2]{0,1:T(2,128)S(1)}, bf16[16,8,20480]{2,1,0:T(8,128)(2,1)}, s32[]{:T(128)}) %tuple.24), condition=%wide.while_cond, body=%wide.while_body.sunk | while | flops 2 | bytes 655973 | solution.py:36
  14.9 0.1 constant_dynamic-slice_fusion.2
  15.0 0.5 slice.24
  15.5 1.5 %bitcast_dynamic-update-slice_fusion.2 = bf16[16,8,20480]{2,1,0:T(8,128)(2,1)} fusion(bf16[16,8,20480]{2,1,0:T(8,128)(2,1)} %get-tuple-element.58, s32[]{:T(128)S(6)} %copy.32, bf16[8,20736]{1,0:T(8,128)(2,1)S(1)} %get-tuple-element.61, s32[]{:T(128)} %bitcast.41), kind=kLoop, calls=%fused_computation.clone.1 | loop fusion | bytes 655876 | tf_op jit(solution)/shard_map/vmap()/gather
  17.0 0.1 constant_dynamic-slice_fusion.2
  17.1 0.5 slice.24
  17.6 1.5 %bitcast_dynamic-update-slice_fusion.2 = bf16[16,8,20480]{2,1,0:T(8,128)(2,1)} fusion(bf16[16,8,20480]{2,1,0:T(8,128)(2,1)} %get-tuple-element.58, s32[]{:T(128)S(6)} %copy.32, bf16[8,20736]{1,0:T(8,128)(2,1)S(1)} %get-tuple-element.61, s32[]{:T(128)} %bitcast.41), kind=kLoop, calls=%fused_computation.clone.1 | loop fusion | bytes 655876 | tf_op jit(solution)/shard_map/vmap()/gather
  19.2 0.1 constant_dynamic-slice_fusion.2
  19.2 0.5 slice.24
  19.8 1.5 %bitcast_dynamic-update-slice_fusion.2 = bf16[16,8,20480]{2,1,0:T(8,128)(2,1)} fusion(bf16[16,8,20480]{2,1,0:T(8,128)(2,1)} %get-tuple-element.58, s32[]{:T(128)S(6)} %copy.32, bf16[8,20736]{1,0:T(8,128)(2,1)S(1)} %get-tuple-element.61, s32[]{:T(128)} %bitcast.41), kind=kLoop, calls=%fused_computation.clone.1 | loop fusion | bytes 655876 | tf_op jit(solution)/shard_map/vmap()/gather
  21.3 0.1 constant_dynamic-slice_fusion.2
  21.4 0.5 slice.24
  21.9 1.5 %bitcast_dynamic-update-slice_fusion.2 = bf16[16,8,20480]{2,1,0:T(8,128)(2,1)} fusion(bf16[16,8,20480]{2,1,0:T(8,128)(2,1)} %get-tuple-element.58, s32[]{:T(128)S(6)} %copy.32, bf16[8,20736]{1,0:T(8,128)(2,1)S(1)} %get-tuple-element.61, s32[]{:T(128)} %bitcast.41), kind=kLoop, calls=%fused_computation.clone.1 | loop fusion | bytes 655876 | tf_op jit(solution)/shard_map/vmap()/gather
  23.4 0.1 constant_dynamic-slice_fusion.2
  23.5 0.5 slice.24
  24.0 1.5 %bitcast_dynamic-update-slice_fusion.2 = bf16[16,8,20480]{2,1,0:T(8,128)(2,1)} fusion(bf16[16,8,20480]{2,1,0:T(8,128)(2,1)} %get-tuple-element.58, s32[]{:T(128)S(6)} %copy.32, bf16[8,20736]{1,0:T(8,128)(2,1)S(1)} %get-tuple-element.61, s32[]{:T(128)} %bitcast.41), kind=kLoop, calls=%fused_computation.clone.1 | loop fusion | bytes 655876 | tf_op jit(solution)/shard_map/vmap()/gather
  25.5 0.1 constant_dynamic-slice_fusion.2
  25.6 0.5 slice.24
  26.1 1.5 %bitcast_dynamic-update-slice_fusion.2 = bf16[16,8,20480]{2,1,0:T(8,128)(2,1)} fusion(bf16[16,8,20480]{2,1,0:T(8,128)(2,1)} %get-tuple-element.58, s32[]{:T(128)S(6)} %copy.32, bf16[8,20736]{1,0:T(8,128)(2,1)S(1)} %get-tuple-element.61, s32[]{:T(128)} %bitcast.41), kind=kLoop, calls=%fused_computation.clone.1 | loop fusion | bytes 655876 | tf_op jit(solution)/shard_map/vmap()/gather
  27.7 0.1 constant_dynamic-slice_fusion.2
  27.7 0.5 slice.24
  28.2 1.6 %bitcast_dynamic-update-slice_fusion.2 = bf16[16,8,20480]{2,1,0:T(8,128)(2,1)} fusion(bf16[16,8,20480]{2,1,0:T(8,128)(2,1)} %get-tuple-element.58, s32[]{:T(128)S(6)} %copy.32, bf16[8,20736]{1,0:T(8,128)(2,1)S(1)} %get-tuple-element.61, s32[]{:T(128)} %bitcast.41), kind=kLoop, calls=%fused_computation.clone.1 | loop fusion | bytes 655876 | tf_op jit(solution)/shard_map/vmap()/gather
  29.8 0.1 constant_dynamic-slice_fusion.2
  29.9 0.5 slice.24
  30.4 1.5 %bitcast_dynamic-update-slice_fusion.2 = bf16[16,8,20480]{2,1,0:T(8,128)(2,1)} fusion(bf16[16,8,20480]{2,1,0:T(8,128)(2,1)} %get-tuple-element.58, s32[]{:T(128)S(6)} %copy.32, bf16[8,20736]{1,0:T(8,128)(2,1)S(1)} %get-tuple-element.61, s32[]{:T(128)} %bitcast.41), kind=kLoop, calls=%fused_computation.clone.1 | loop fusion | bytes 655876 | tf_op jit(solution)/shard_map/vmap()/gather
  31.9 0.1 constant_dynamic-slice_fusion.2
  32.0 0.5 slice.24
  32.5 1.5 %bitcast_dynamic-update-slice_fusion.2 = bf16[16,8,20480]{2,1,0:T(8,128)(2,1)} fusion(bf16[16,8,20480]{2,1,0:T(8,128)(2,1)} %get-tuple-element.58, s32[]{:T(128)S(6)} %copy.32, bf16[8,20736]{1,0:T(8,128)(2,1)S(1)} %get-tuple-element.61, s32[]{:T(128)} %bitcast.41), kind=kLoop, calls=%fused_computation.clone.1 | loop fusion | bytes 655876 | tf_op jit(solution)/shard_map/vmap()/gather
  34.0 0.1 constant_dynamic-slice_fusion.2
  34.1 0.5 slice.24
  34.6 1.5 %bitcast_dynamic-update-slice_fusion.2 = bf16[16,8,20480]{2,1,0:T(8,128)(2,1)} fusion(bf16[16,8,20480]{2,1,0:T(8,128)(2,1)} %get-tuple-element.58, s32[]{:T(128)S(6)} %copy.32, bf16[8,20736]{1,0:T(8,128)(2,1)S(1)} %get-tuple-element.61, s32[]{:T(128)} %bitcast.41), kind=kLoop, calls=%fused_computation.clone.1 | loop fusion | bytes 655876 | tf_op jit(solution)/shard_map/vmap()/gather
  36.2 0.1 constant_dynamic-slice_fusion.2
  36.2 0.5 slice.24
  36.8 1.5 %bitcast_dynamic-update-slice_fusion.2 = bf16[16,8,20480]{2,1,0:T(8,128)(2,1)} fusion(bf16[16,8,20480]{2,1,0:T(8,128)(2,1)} %get-tuple-element.58, s32[]{:T(128)S(6)} %copy.32, bf16[8,20736]{1,0:T(8,128)(2,1)S(1)} %get-tuple-element.61, s32[]{:T(128)} %bitcast.41), kind=kLoop, calls=%fused_computation.clone.1 | loop fusion | bytes 655876 | tf_op jit(solution)/shard_map/vmap()/gather
  38.4 0.5 slice.24
  38.9 1.5 %bitcast_dynamic-update-slice_fusion.2 = bf16[16,8,20480]{2,1,0:T(8,128)(2,1)} fusion(bf16[16,8,20480]{2,1,0:T(8,128)(2,1)} %get-tuple-element.58, s32[]{:T(128)S(6)} %copy.32, bf16[8,20736]{1,0:T(8,128)(2,1)S(1)} %get-tuple-element.61, s32[]{:T(128)} %bitcast.41), kind=kLoop, calls=%fused_computation.clone.1 | loop fusion | bytes 655876 | tf_op jit(solution)/shard_map/vmap()/gather
  40.5 0.5 slice.24
  41.0 1.5 %bitcast_dynamic-update-slice_fusion.2 = bf16[16,8,20480]{2,1,0:T(8,128)(2,1)} fusion(bf16[16,8,20480]{2,1,0:T(8,128)(2,1)} %get-tuple-element.58, s32[]{:T(128)S(6)} %copy.32, bf16[8,20736]{1,0:T(8,128)(2,1)S(1)} %get-tuple-element.61, s32[]{:T(128)} %bitcast.41), kind=kLoop, calls=%fused_computation.clone.1 | loop fusion | bytes 655876 | tf_op jit(solution)/shard_map/vmap()/gather
  42.6 0.5 slice.24
  43.1 1.5 %bitcast_dynamic-update-slice_fusion.2 = bf16[16,8,20480]{2,1,0:T(8,128)(2,1)} fusion(bf16[16,8,20480]{2,1,0:T(8,128)(2,1)} %get-tuple-element.58, s32[]{:T(128)S(6)} %copy.32, bf16[8,20736]{1,0:T(8,128)(2,1)S(1)} %get-tuple-element.61, s32[]{:T(128)} %bitcast.41), kind=kLoop, calls=%fused_computation.clone.1 | loop fusion | bytes 655876 | tf_op jit(solution)/shard_map/vmap()/gather
  44.7 0.5 slice.24
  45.2 1.5 %bitcast_dynamic-update-slice_fusion.2 = bf16[16,8,20480]{2,1,0:T(8,128)(2,1)} fusion(bf16[16,8,20480]{2,1,0:T(8,128)(2,1)} %get-tuple-element.58, s32[]{:T(128)S(6)} %copy.32, bf16[8,20736]{1,0:T(8,128)(2,1)S(1)} %get-tuple-element.61, s32[]{:T(128)} %bitcast.41), kind=kLoop, calls=%fused_computation.clone.1 | loop fusion | bytes 655876 | tf_op jit(solution)/shard_map/vmap()/gather
  46.8 0.5 slice.24
  47.3 1.5 %bitcast_dynamic-update-slice_fusion.2 = bf16[16,8,20480]{2,1,0:T(8,128)(2,1)} fusion(bf16[16,8,20480]{2,1,0:T(8,128)(2,1)} %get-tuple-element.58, s32[]{:T(128)S(6)} %copy.32, bf16[8,20736]{1,0:T(8,128)(2,1)S(1)} %get-tuple-element.61, s32[]{:T(128)} %bitcast.41), kind=kLoop, calls=%fused_computation.clone.1 | loop fusion | bytes 655876 | tf_op jit(solution)/shard_map/vmap()/gather
  48.9 0.3 copy.22
  49.2 1.2 %fusion.36 = (bf16[48,159,128]{2,1,0:T(8,128)(2,1)S(1)}, bf16[48,159,128]{2,1,0:T(8,128)(2,1)S(1)}) fusion(bf16[48,160,128]{2,1,0:T(8,128)(2,1)S(1)} %bitcast.42), kind=kLoop, calls=%fused_computation.47 | loop fusion | bytes 7815168 | tf_op jit(solution)/shard_map/slice | solution.py:23
  50.4 3.1 %subtract_convert_fusion = bf16[48,160,128]{2,1,0:T(8,128)(2,1)} fusion(bf16[48,160,128]{2,1,0:T(8,128)(2,1)S(1)} %bitcast.43, bf16[48,159,128]{2,1,0:T(8,128)(2,1)S(1)} %get-tuple-element.23, bf16[48,159,128]{2,1,0:T(8,128)(2,1)S(1)} %get-tuple-element.22, s32[384]{0:T(512)S(1)} %iota_add_fusion), kind=kOutput, calls=%fused_computation.16 | convolution fusion | flops 788643840 | bytes 7841280 | tf_op jit(solution)/shard_map/rbj,ji->rbi/dot_general | solution.py:26
  53.5 3.7 %dot_general.9 = bf16[8,6,20480]{2,1,0:T(8,128)(2,1)S(1)} reshape(bf16[48,160,128]{2,1,0:T(8,128)(2,1)} %subtract_convert_fusion) | data formatting | bytes 3932160 | tf_op jit(solution)/shard_map/mb,sb->ms/dot_general | solution.py:53
  57.3 13.3 %fusion.12 = f32[8,16,8,6]{2,0,3,1:T(8,128)S(1)} fusion(bf16[16,8,20480]{2,1,0:T(8,128)(2,1)} %get-tuple-element.9, bf16[8,6,20480]{2,1,0:T(8,128)(2,1)S(1)} %dot_general.9), kind=kOutput, calls=%fused_computation.14 | convolution fusion | flops 251658240 | bytes 7233536 | tf_op jit(solution)/shard_map/mb,sb->ms/dot_general | solution.py:53
  70.6 0.2 copy.19
  70.8 0.7 reshape.74
  71.6 4.9 %all-to-all-start = ((f32[8,1,768]{2,1,0:T(1,128)}), f32[8,1,768]{2,1,0:T(1,128)S(1)}, u32[]{:S(2)}, u32[]{:S(2)}) async-start(f32[8,1,768]{2,1,0:T(1,128)} %reshape.74), calls=%async_computation | async-start | bytes 49152 | tf_op jit(solution)/shard_map/all_to_all | solution.py:58
  76.5 0.1 dynamic-slice_add_fusion
  76.6 0.1 compare_and_fusion
  76.6 5.5 %all-to-all-done = f32[8,1,768]{2,1,0:T(1,128)S(1)} async-done(((f32[8,1,768]{2,1,0:T(1,128)}), f32[8,1,768]{2,1,0:T(1,128)S(1)}, u32[]{:S(2)}, u32[]{:S(2)}) %all-to-all-start) | async-done | bytes 24608 | tf_op jit(solution)/shard_map/all_to_all | solution.py:58
  82.2 0.5 broadcast.91
  82.7 0.7 reduce.2
  83.4 0.1 reshape.75
  83.5 0.7 fusion.20
  84.2 0.7 divide_bitcast_fusion
  (16 shorter events, 0.4 us)
Async XLA Ops:
  0.6 48.3 %copy-start = (bf16[48,20480]{1,0:T(8,128)(2,1)S(1)}, bf16[48,20480]{1,0:T(8,128)(2,1)}, u32[]{:S(2)}) copy-start(bf16[48,20480]{1,0:T(8,128)(2,1)} %param.5) | copy-start | bytes 5898244
  57.2 19.2 %copy-start.1 = (s32[48]{0:T(128)S(1)}, s32[48]{0:T(128)}, u32[]{:S(2)}) copy-start(s32[48]{0:T(128)} %param.9) | copy-start | bytes 580
  57.3 19.2 %copy-start.2 = (s32[48]{0:T(128)S(1)}, s32[48]{0:T(128)}, u32[]{:S(2)}) copy-start(s32[48]{0:T(128)} %param.8) | copy-start | bytes 580
  71.6 10.6 %all-to-all-start = ((f32[8,1,768]{2,1,0:T(1,128)}), f32[8,1,768]{2,1,0:T(1,128)S(1)}, u32[]{:S(2)}, u32[]{:S(2)}) async-start(f32[8,1,768]{2,1,0:T(1,128)} %reshape.74), calls=%async_computation | async-start | bytes 49152 | tf_op jit(solution)/shard_map/all_to_all | solution.py:58
where the time goes:
time: 85.3 us; the launch traced here: 84.9 us
  local copies, waits for them, and re-layouts  42.3 us (50%)
  matrix products  16.4 us (19%)
  blocking collectives  12 us (14%)
  waiting for transfers between devices  5.51 us (6%)
  starting transfers between devices  4.88 us (6%)
  other arithmetic  2.93 us (3%)
    gather x48, local copies, waits for them, and re-layouts  33.9 us
    dot_general x1, matrix products, local(): jnp.einsum('mb,sb->ms', copies, corrected, preferred_element_type=jnp.flo...  13.3 us
    all_gather x1, blocking collectives, local(): piece = lax.all_gather(theo, 'band', axis=1, tiled=True)  12 us
    all_to_all x1, waiting for transfers between devices, local(): lax.all_to_all(score_table, 'query', split_axis=2, concat_axis=0, tiled=T...  5.51 us
    all_to_all x1, starting transfers between devices, local(): lax.all_to_all(score_table, 'query', split_axis=2, concat_axis=0, tiled=T...  4.88 us
    dot_general x2, local copies, waits for them, and re-layouts, local(): jnp.einsum('mb,sb->ms', copies, corrected, preferred_element_type=jnp.flo...  3.95 us
    dot_general x1, matrix products, correct(): jnp.einsum('rbj,ji->rbi', stacked, box_table(), preferred_element_type=jn...  3.08 us
    unnamed x11, local copies, waits for them, and re-layouts  2.71 us
  transfers between devices with their start and end apart: 1, of which 1 were waited for; matrix products, arithmetic and copies ran while one was open for 0% of the time, Pallas kernels for 0%

commit v1 on v0

--- a/solution.py
+++ b/solution.py
@@ -55,7 +55,17 @@
     score_table = scores.reshape(group_size, shift_count, query_count, own_rows)
     low_own = lax.dynamic_slice_in_dim(win_lo, own_start, own_rows, 0)
     length_own = lax.dynamic_slice_in_dim(win_len, own_start, own_rows, 0)
-    gathered = lax.all_to_all(score_table, "query", split_axis=2, concat_axis=0, tiled=True)
+    r2, right_arr = (lax.axis_size("query"), lax.axis_index("query"))
+    taken_in = score_table.shape[2] // r2
+    t1 = jnp.roll(score_table, -right_arr * taken_in, axis=2)
+    store = [lax.slice_in_dim(t1, 0, taken_in, axis=2)]
+    q = 1
+    while q < r2:
+        x_now = lax.slice_in_dim(t1, q * taken_in, (q + 1) * taken_in, axis=2)
+        store.append(lax.ppermute(x_now, "query", perm=[(w, (w + q) % r2) for w in range(r2)]))
+        q = q + 1
+    res = jnp.concatenate(store[::-1], 0)
+    gathered = jnp.roll(res, (right_arr + 1) * store[0].shape[0], axis=0)
     total_peptides = gathered.shape[0]
     owned_scores = gathered.reshape(total_peptides, shift_count, own_rows)
     peptide_index = lax.broadcasted_iota(jnp.int32, (total_peptides, own_rows), 0)

time: 85.3 us -> 150 us (1.76)
  waiting for transfers between devices: 5.51 us -> 56.9 us
  local copies, waits for them, and re-layouts: 42.3 us -> 51.8 us
  starting transfers between devices: 4.88 us -> 9.12 us
    ppermute x0 -> x7, waiting for transfers between devices: none -> 56.9 us  [local(): lax.ppermute(x_now, 'query', perm=[(w, (w + q) % r2) for w in range(r2)])]
    ppermute x0 -> x7, local copies, waits for them, and re-layouts: none -> 9.38 us  [local(): lax.ppermute(x_now, 'query', perm=[(w, (w + q) % r2) for w in range(r2)])]
    ppermute x0 -> x7, starting transfers between devices: none -> 9.12 us  [local(): lax.ppermute(x_now, 'query', perm=[(w, (w + q) % r2) for w in range(r2)])]
    all_to_all x1 -> x0, waiting for transfers between devices: 5.51 us -> none  [local(): lax.all_to_all(score_table, 'query', split_axis=2, concat_axis=0, tiled=T...]
    all_to_all x1 -> x0, starting transfers between devices: 4.88 us -> none  [local(): lax.all_to_all(score_table, 'query', split_axis=2, concat_axis=0, tiled=T...]
    dot_general x2 -> x1, local copies, waits for them, and re-layouts: 3.95 us -> 3.71 us  [local(): jnp.einsum('mb,sb->ms', copies, corrected, preferred_element_type=jnp.flo...]
  transfers between devices with their start and end apart: 1 -> 7, of which waited for: 1 -> 4; matrix products, arithmetic and copies ran while one was open for 0% -> 6% of each run, Pallas kernels for 0% -> 0%
where the time goes in v1:
time: 150 us
  waiting for transfers between devices  56.9 us (38%)
  local copies, waits for them, and re-layouts  51.8 us (35%)
  matrix products  16.4 us (11%)
  blocking collectives  12 us (8%)
  starting transfers between devices  9.12 us (6%)
  other arithmetic  2.53 us (2%)
    ppermute x7, waiting for transfers between devices, local(): lax.ppermute(x_now, 'query', perm=[(w, (w + q) % r2) for w in range(r2)])  56.9 us
    gather x48, local copies, waits for them, and re-layouts  33.9 us
    dot_general x1, matrix products, local(): jnp.einsum('mb,sb->ms', copies, corrected, preferred_element_type=jnp.flo...  13.3 us
    all_gather x1, blocking collectives, local(): piece = lax.all_gather(theo, 'band', axis=1, tiled=True)  12 us
    ppermute x7, local copies, waits for them, and re-layouts, local(): lax.ppermute(x_now, 'query', perm=[(w, (w + q) % r2) for w in range(r2)])  9.38 us
    ppermute x7, starting transfers between devices, local(): lax.ppermute(x_now, 'query', perm=[(w, (w + q) % r2) for w in range(r2)])  9.12 us
    dot_general x1, local copies, waits for them, and re-layouts, local(): jnp.einsum('mb,sb->ms', copies, corrected, preferred_element_type=jnp.flo...  3.71 us
    dot_general x1, matrix products, correct(): jnp.einsum('rbj,ji->rbi', stacked, box_table(), preferred_element_type=jn...  3.09 us
  transfers between devices with their start and end apart: 7, of which 4 were waited for; matrix products, arithmetic and copies ran while one was open for 6% of the time, Pallas kernels for 0%

profile of v1, /device:TPU:0, one launch (start us, length us, event | category | flops | bytes accessed | tf_op | source)
XLA Modules:
  0.0 149.6 jit_solution(16308068733184761514)
XLA Ops:
  0.7 1.1 copy.30
  1.8 12.0 %all_gather.3 = bf16[1,8,20480]{2,0,1:T(2,128)(2,1)S(1)} all-gather(bf16[1,2,20480]{2,0,1:T(2,128)(2,1)S(1)} %copy.30), channel_id=1, replica_groups=mesh['band'=4,'query'=8] {'band'}, dimensions={1}, use_global_device_ids=true | all-gather | bytes 409600 | tf_op jit(solution)/shard_map/all_gather | solution.py:50
  13.9 0.4 copy.56
  14.2 0.7 fusion.31
  14.9 34.0 %while.1 = (s32[]{:T(128)}, bf16[8,20736]{1,0:T(8,128)(2,1)S(1)}, s32[16,2]{0,1:T(2,128)S(1)}, bf16[16,8,20480]{2,1,0:T(8,128)(2,1)}, s32[]{:T(128)}) while((s32[]{:T(128)}, bf16[8,20736]{1,0:T(8,128)(2,1)S(1)}, s32[16,2]{0,1:T(2,128)S(1)}, bf16[16,8,20480]{2,1,0:T(8,128)(2,1)}, s32[]{:T(128)}) %tuple.31), condition=%wide.while_cond, body=%wide.while_body.sunk | while | flops 2 | bytes 655973 | solution.py:36
  15.0 0.5 slice.72
  15.5 1.5 %bitcast_dynamic-update-slice_fusion.2 = bf16[16,8,20480]{2,1,0:T(8,128)(2,1)} fusion(bf16[16,8,20480]{2,1,0:T(8,128)(2,1)} %get-tuple-element.66, s32[]{:T(128)S(6)} %copy.60, bf16[8,20736]{1,0:T(8,128)(2,1)S(1)} %get-tuple-element.69, s32[]{:T(128)} %bitcast.36), kind=kLoop, calls=%fused_computation.clone.1 | loop fusion | bytes 655876 | tf_op jit(solution)/shard_map/vmap()/gather
  17.1 0.5 slice.72
  17.7 1.5 %bitcast_dynamic-update-slice_fusion.2 = bf16[16,8,20480]{2,1,0:T(8,128)(2,1)} fusion(bf16[16,8,20480]{2,1,0:T(8,128)(2,1)} %get-tuple-element.66, s32[]{:T(128)S(6)} %copy.60, bf16[8,20736]{1,0:T(8,128)(2,1)S(1)} %get-tuple-element.69, s32[]{:T(128)} %bitcast.36), kind=kLoop, calls=%fused_computation.clone.1 | loop fusion | bytes 655876 | tf_op jit(solution)/shard_map/vmap()/gather
  19.3 0.5 slice.72
  19.8 1.5 %bitcast_dynamic-update-slice_fusion.2 = bf16[16,8,20480]{2,1,0:T(8,128)(2,1)} fusion(bf16[16,8,20480]{2,1,0:T(8,128)(2,1)} %get-tuple-element.66, s32[]{:T(128)S(6)} %copy.60, bf16[8,20736]{1,0:T(8,128)(2,1)S(1)} %get-tuple-element.69, s32[]{:T(128)} %bitcast.36), kind=kLoop, calls=%fused_computation.clone.1 | loop fusion | bytes 655876 | tf_op jit(solution)/shard_map/vmap()/gather
  21.4 0.5 slice.72
  21.9 1.5 %bitcast_dynamic-update-slice_fusion.2 = bf16[16,8,20480]{2,1,0:T(8,128)(2,1)} fusion(bf16[16,8,20480]{2,1,0:T(8,128)(2,1)} %get-tuple-element.66, s32[]{:T(128)S(6)} %copy.60, bf16[8,20736]{1,0:T(8,128)(2,1)S(1)} %get-tuple-element.69, s32[]{:T(128)} %bitcast.36), kind=kLoop, calls=%fused_computation.clone.1 | loop fusion | bytes 655876 | tf_op jit(solution)/shard_map/vmap()/gather
  23.5 0.5 slice.72
  24.0 1.5 %bitcast_dynamic-update-slice_fusion.2 = bf16[16,8,20480]{2,1,0:T(8,128)(2,1)} fusion(bf16[16,8,20480]{2,1,0:T(8,128)(2,1)} %get-tuple-element.66, s32[]{:T(128)S(6)} %copy.60, bf16[8,20736]{1,0:T(8,128)(2,1)S(1)} %get-tuple-element.69, s32[]{:T(128)} %bitcast.36), kind=kLoop, calls=%fused_computation.clone.1 | loop fusion | bytes 655876 | tf_op jit(solution)/shard_map/vmap()/gather
  25.6 0.5 slice.72
  26.1 1.5 %bitcast_dynamic-update-slice_fusion.2 = bf16[16,8,20480]{2,1,0:T(8,128)(2,1)} fusion(bf16[16,8,20480]{2,1,0:T(8,128)(2,1)} %get-tuple-element.66, s32[]{:T(128)S(6)} %copy.60, bf16[8,20736]{1,0:T(8,128)(2,1)S(1)} %get-tuple-element.69, s32[]{:T(128)} %bitcast.36), kind=kLoop, calls=%fused_computation.clone.1 | loop fusion | bytes 655876 | tf_op jit(solution)/shard_map/vmap()/gather
  27.7 0.5 slice.72
  28.2 1.6 %bitcast_dynamic-update-slice_fusion.2 = bf16[16,8,20480]{2,1,0:T(8,128)(2,1)} fusion(bf16[16,8,20480]{2,1,0:T(8,128)(2,1)} %get-tuple-element.66, s32[]{:T(128)S(6)} %copy.60, bf16[8,20736]{1,0:T(8,128)(2,1)S(1)} %get-tuple-element.69, s32[]{:T(128)} %bitcast.36), kind=kLoop, calls=%fused_computation.clone.1 | loop fusion | bytes 655876 | tf_op jit(solution)/shard_map/vmap()/gather
  29.9 0.5 slice.72
  30.4 1.5 %bitcast_dynamic-update-slice_fusion.2 = bf16[16,8,20480]{2,1,0:T(8,128)(2,1)} fusion(bf16[16,8,20480]{2,1,0:T(8,128)(2,1)} %get-tuple-element.66, s32[]{:T(128)S(6)} %copy.60, bf16[8,20736]{1,0:T(8,128)(2,1)S(1)} %get-tuple-element.69, s32[]{:T(128)} %bitcast.36), kind=kLoop, calls=%fused_computation.clone.1 | loop fusion | bytes 655876 | tf_op jit(solution)/shard_map/vmap()/gather
  32.0 0.5 slice.72
  32.5 1.5 %bitcast_dynamic-update-slice_fusion.2 = bf16[16,8,20480]{2,1,0:T(8,128)(2,1)} fusion(bf16[16,8,20480]{2,1,0:T(8,128)(2,1)} %get-tuple-element.66, s32[]{:T(128)S(6)} %copy.60, bf16[8,20736]{1,0:T(8,128)(2,1)S(1)} %get-tuple-element.69, s32[]{:T(128)} %bitcast.36), kind=kLoop, calls=%fused_computation.clone.1 | loop fusion | bytes 655876 | tf_op jit(solution)/shard_map/vmap()/gather
  34.1 0.5 slice.72
  34.6 1.5 %bitcast_dynamic-update-slice_fusion.2 = bf16[16,8,20480]{2,1,0:T(8,128)(2,1)} fusion(bf16[16,8,20480]{2,1,0:T(8,128)(2,1)} %get-tuple-element.66, s32[]{:T(128)S(6)} %copy.60, bf16[8,20736]{1,0:T(8,128)(2,1)S(1)} %get-tuple-element.69, s32[]{:T(128)} %bitcast.36), kind=kLoop, calls=%fused_computation.clone.1 | loop fusion | bytes 655876 | tf_op jit(solution)/shard_map/vmap()/gather
  36.3 0.5 slice.72
  36.8 1.5 %bitcast_dynamic-update-slice_fusion.2 = bf16[16,8,20480]{2,1,0:T(8,128)(2,1)} fusion(bf16[16,8,20480]{2,1,0:T(8,128)(2,1)} %get-tuple-element.66, s32[]{:T(128)S(6)} %copy.60, bf16[8,20736]{1,0:T(8,128)(2,1)S(1)} %get-tuple-element.69, s32[]{:T(128)} %bitcast.36), kind=kLoop, calls=%fused_computation.clone.1 | loop fusion | bytes 655876 | tf_op jit(solution)/shard_map/vmap()/gather
  38.4 0.5 slice.72
  38.9 1.5 %bitcast_dynamic-update-slice_fusion.2 = bf16[16,8,20480]{2,1,0:T(8,128)(2,1)} fusion(bf16[16,8,20480]{2,1,0:T(8,128)(2,1)} %get-tuple-element.66, s32[]{:T(128)S(6)} %copy.60, bf16[8,20736]{1,0:T(8,128)(2,1)S(1)} %get-tuple-element.69, s32[]{:T(128)} %bitcast.36), kind=kLoop, calls=%fused_computation.clone.1 | loop fusion | bytes 655876 | tf_op jit(solution)/shard_map/vmap()/gather
  40.5 0.5 slice.72
  41.0 1.5 %bitcast_dynamic-update-slice_fusion.2 = bf16[16,8,20480]{2,1,0:T(8,128)(2,1)} fusion(bf16[16,8,20480]{2,1,0:T(8,128)(2,1)} %get-tuple-element.66, s32[]{:T(128)S(6)} %copy.60, bf16[8,20736]{1,0:T(8,128)(2,1)S(1)} %get-tuple-element.69, s32[]{:T(128)} %bitcast.36), kind=kLoop, calls=%fused_computation.clone.1 | loop fusion | bytes 655876 | tf_op jit(solution)/shard_map/vmap()/gather
  42.6 0.5 slice.72
  43.1 1.5 %bitcast_dynamic-update-slice_fusion.2 = bf16[16,8,20480]{2,1,0:T(8,128)(2,1)} fusion(bf16[16,8,20480]{2,1,0:T(8,128)(2,1)} %get-tuple-element.66, s32[]{:T(128)S(6)} %copy.60, bf16[8,20736]{1,0:T(8,128)(2,1)S(1)} %get-tuple-element.69, s32[]{:T(128)} %bitcast.36), kind=kLoop, calls=%fused_computation.clone.1 | loop fusion | bytes 655876 | tf_op jit(solution)/shard_map/vmap()/gather
  44.7 0.5 slice.72
  45.2 1.5 %bitcast_dynamic-update-slice_fusion.2 = bf16[16,8,20480]{2,1,0:T(8,128)(2,1)} fusion(bf16[16,8,20480]{2,1,0:T(8,128)(2,1)} %get-tuple-element.66, s32[]{:T(128)S(6)} %copy.60, bf16[8,20736]{1,0:T(8,128)(2,1)S(1)} %get-tuple-element.69, s32[]{:T(128)} %bitcast.36), kind=kLoop, calls=%fused_computation.clone.1 | loop fusion | bytes 655876 | tf_op jit(solution)/shard_map/vmap()/gather
  46.9 0.5 slice.72
  47.4 1.5 %bitcast_dynamic-update-slice_fusion.2 = bf16[16,8,20480]{2,1,0:T(8,128)(2,1)} fusion(bf16[16,8,20480]{2,1,0:T(8,128)(2,1)} %get-tuple-element.66, s32[]{:T(128)S(6)} %copy.60, bf16[8,20736]{1,0:T(8,128)(2,1)S(1)} %get-tuple-element.69, s32[]{:T(128)} %bitcast.36), kind=kLoop, calls=%fused_computation.clone.1 | loop fusion | bytes 655876 | tf_op jit(solution)/shard_map/vmap()/gather
  48.9 0.3 copy.50
  49.2 1.2 fusion.37
  50.4 3.1 %subtract_convert_fusion = bf16[48,160,128]{2,1,0:T(8,128)(2,1)} fusion(bf16[48,160,128]{2,1,0:T(8,128)(2,1)S(1)} %bitcast.38, bf16[48,159,128]{2,1,0:T(8,128)(2,1)S(1)} %get-tuple-element.23, bf16[48,159,128]{2,1,0:T(8,128)(2,1)S(1)} %get-tuple-element.22, s32[384]{0:T(512)S(1)} %iota_add_fusion), kind=kOutput, calls=%fused_computation.16 | convolution fusion | flops 788643840 | bytes 7841280 | tf_op jit(solution)/shard_map/rbj,ji->rbi/dot_general | solution.py:26
  53.5 3.7 %dot_general.9 = bf16[8,6,20480]{2,1,0:T(8,128)(2,1)S(1)} reshape(bf16[48,160,128]{2,1,0:T(8,128)(2,1)} %subtract_convert_fusion) | data formatting | bytes 3932160 | tf_op jit(solution)/shard_map/mb,sb->ms/dot_general | solution.py:53
  57.3 13.3 %fusion.12 = f32[8,16,8,6]{2,0,3,1:T(8,128)S(1)} fusion(bf16[16,8,20480]{2,1,0:T(8,128)(2,1)} %get-tuple-element.9, bf16[8,6,20480]{2,1,0:T(8,128)(2,1)S(1)} %dot_general.9), kind=kOutput, calls=%fused_computation.14 | convolution fusion | flops 251658240 | bytes 7233536 | tf_op jit(solution)/shard_map/mb,sb->ms/dot_general | solution.py:53
  70.6 0.3 dynamic-slice_maximum_fusion
  70.9 0.8 fusion.38
  71.7 1.1 collective-permute-start
  72.8 2.6 %collective-permute-start.1 = (f32[8,16,1,6]{2,0,3,1:T(8,128)S(1)}, f32[8,16,1,6]{2,0,3,1:T(8,128)}, u32[]{:S(2)}, u32[]{:S(2)}) collective-permute-start(f32[8,16,1,6]{2,0,3,1:T(8,128)S(1)} %get-tuple-element.30), channel_id=1, source_target_pairs={{0,6},{1,7},{2,0},{3,1},{4,2},{5,3},{6,4},{7,5},{8,14},{9,15},{10,... | collective-permute-start | bytes 9224 | tf_op jit(solution)/shard_map/ppermute | solution.py:65
  75.4 2.7 %collective-permute-start.3 = (f32[8,16,1,6]{2,0,3,1:T(8,128)S(1)}, f32[8,16,1,6]{2,0,3,1:T(8,128)}, u32[]{:S(2)}, u32[]{:S(2)}) collective-permute-start(f32[8,16,1,6]{2,0,3,1:T(8,128)S(1)} %get-tuple-element.28), channel_id=1, source_target_pairs={{0,4},{1,5},{2,6},{3,7},{4,0},{5,1},{6,2},{7,3},{8,12},{9,13},{10,... | collective-permute-start | bytes 9224 | tf_op jit(solution)/shard_map/ppermute | solution.py:65
  78.1 0.1 dynamic-slice_add_fusion
  78.2 1.9 %collective-permute-done = f32[8,16,1,6]{2,0,3,1:T(8,128)} collective-permute-done((f32[8,16,1,6]{2,0,3,1:T(8,128)S(1)}, f32[8,16,1,6]{2,0,3,1:T(8,128)}, u32[]{:S(2)}, u32[]{:S(2)}) %collective-permute-start) | collective-permute-done | bytes 3104 | tf_op jit(solution)/shard_map/ppermute | solution.py:65
  80.1 2.7 %collective-permute-start.5 = (f32[8,16,1,6]{2,0,3,1:T(8,128)S(1)}, f32[8,16,1,6]{2,0,3,1:T(8,128)S(1)}, u32[]{:S(2)}, u32[]{:S(2)}) collective-permute-start(f32[8,16,1,6]{2,0,3,1:T(8,128)S(1)} %get-tuple-element.26), channel_id=1, source_target_pairs={{0,2},{1,3},{2,4},{3,5},{4,6},{5,7},{6,0},{7,1},{8,10},{9,11},{10,... | collective-permute-start | bytes 9224 | tf_op jit(solution)/shard_map/ppermute | solution.py:65
  82.8 9.0 %collective-permute-done.1 = f32[8,16,1,6]{2,0,3,1:T(8,128)} collective-permute-done((f32[8,16,1,6]{2,0,3,1:T(8,128)S(1)}, f32[8,16,1,6]{2,0,3,1:T(8,128)}, u32[]{:S(2)}, u32[]{:S(2)}) %collective-permute-start.1) | collective-permute-done | bytes 3104 | tf_op jit(solution)/shard_map/ppermute | solution.py:65
  91.9 0.6 copy.39
  92.5 1.6 %copy.32 = f32[8,16,1,6]{0,1,3,2:T(8,128)S(1)} copy(f32[8,16,1,6]{2,0,3,1:T(8,128)} %collective-permute-done) | data formatting | bytes 6144 | tf_op jit(solution)/shard_map/ppermute | solution.py:65
  94.1 1.6 %copy.33 = f32[8,16,1,6]{0,1,3,2:T(8,128)S(1)} copy(f32[8,16,1,6]{2,0,3,1:T(8,128)} %collective-permute-done.1) | data formatting | bytes 6144 | tf_op jit(solution)/shard_map/ppermute | solution.py:65
  95.7 1.3 collective-permute-done.2
  97.0 1.6 %copy.34 = f32[8,16,1,6]{0,1,3,2:T(8,128)S(1)} copy(f32[8,16,1,6]{2,0,3,1:T(8,128)} %collective-permute-done.2) | data formatting | bytes 6144 | tf_op jit(solution)/shard_map/ppermute | solution.py:65
  98.6 44.7 %collective-permute-done.3 = f32[8,16,1,6]{2,0,3,1:T(8,128)} collective-permute-done((f32[8,16,1,6]{2,0,3,1:T(8,128)S(1)}, f32[8,16,1,6]{2,0,3,1:T(8,128)}, u32[]{:S(2)}, u32[]{:S(2)}) %collective-permute-start.3) | collective-permute-done | bytes 3104 | tf_op jit(solution)/shard_map/ppermute | solution.py:65
  143.4 1.6 %copy.35 = f32[8,16,1,6]{0,1,3,2:T(8,128)S(1)} copy(f32[8,16,1,6]{2,0,3,1:T(8,128)} %collective-permute-done.3) | data formatting | bytes 6144 | tf_op jit(solution)/shard_map/ppermute | solution.py:65
  145.0 1.6 %copy.36 = f32[8,16,1,6]{0,1,3,2:T(8,128)S(1)} copy(f32[8,16,1,6]{2,0,3,1:T(8,128)} %collective-permute-done.4) | data formatting | bytes 6144 | tf_op jit(solution)/shard_map/ppermute | solution.py:65
  146.6 0.6 copy.37
  147.2 0.6 copy.38
  147.9 0.3 concatenate.27
  148.2 0.8 fusion.28
  148.9 0.7 divide_bitcast_fusion
  (33 shorter events, 1.3 us)
Async XLA Ops:
  0.6 48.3 %copy-start = (bf16[48,20480]{1,0:T(8,128)(2,1)S(1)}, bf16[48,20480]{1,0:T(8,128)(2,1)}, u32[]{:S(2)}) copy-start(bf16[48,20480]{1,0:T(8,128)(2,1)} %param.5) | copy-start | bytes 5898244
  70.6 7.5 %copy-start.1 = (s32[48]{0:T(128)S(1)}, s32[48]{0:T(128)}, u32[]{:S(2)}) copy-start(s32[48]{0:T(128)} %param.9) | copy-start | bytes 580
  70.6 7.5 %copy-start.2 = (s32[48]{0:T(128)S(1)}, s32[48]{0:T(128)}, u32[]{:S(2)}) copy-start(s32[48]{0:T(128)} %param.8) | copy-start | bytes 580
  71.7 8.4 %collective-permute-start = (f32[8,16,1,6]{2,0,3,1:T(8,128)S(1)}, f32[8,16,1,6]{2,0,3,1:T(8,128)}, u32[]{:S(2)}, u32[]{:S(2)}) collective-permute-start(f32[8,16,1,6]{2,0,3,1:T(8,128)S(1)} %get-tuple-element.31), channel_id=1, source_target_pairs={{0,7},{1,0},{2,1},{3,2},{4,3},{5,4},{6,5},{7,6},{8,15},{9,8},{10,9... | collective-permute-start | bytes 9224 | tf_op jit(solution)/shard_map/ppermute | solution.py:65
  72.8 19.0 %collective-permute-start.1 = (f32[8,16,1,6]{2,0,3,1:T(8,128)S(1)}, f32[8,16,1,6]{2,0,3,1:T(8,128)}, u32[]{:S(2)}, u32[]{:S(2)}) collective-permute-start(f32[8,16,1,6]{2,0,3,1:T(8,128)S(1)} %get-tuple-element.30), channel_id=1, source_target_pairs={{0,6},{1,7},{2,0},{3,1},{4,2},{5,3},{6,4},{7,5},{8,14},{9,15},{10,... | collective-permute-start | bytes 9224 | tf_op jit(solution)/shard_map/ppermute | solution.py:65
  75.4 21.6 %collective-permute-start.2 = (f32[8,16,1,6]{2,0,3,1:T(8,128)S(1)}, f32[8,16,1,6]{2,0,3,1:T(8,128)}, u32[]{:S(2)}, u32[]{:S(2)}) collective-permute-start(f32[8,16,1,6]{2,0,3,1:T(8,128)S(1)} %get-tuple-element.29), channel_id=1, source_target_pairs={{0,5},{1,6},{2,7},{3,0},{4,1},{5,2},{6,3},{7,4},{8,13},{9,14},{10,... | collective-permute-start | bytes 9224 | tf_op jit(solution)/shard_map/ppermute | solution.py:65
  75.4 68.0 %collective-permute-start.3 = (f32[8,16,1,6]{2,0,3,1:T(8,128)S(1)}, f32[8,16,1,6]{2,0,3,1:T(8,128)}, u32[]{:S(2)}, u32[]{:S(2)}) collective-permute-start(f32[8,16,1,6]{2,0,3,1:T(8,128)S(1)} %get-tuple-element.28), channel_id=1, source_target_pairs={{0,4},{1,5},{2,6},{3,7},{4,0},{5,1},{6,2},{7,3},{8,12},{9,13},{10,... | collective-permute-start | bytes 9224 | tf_op jit(solution)/shard_map/ppermute | solution.py:65
  78.1 66.9 %collective-permute-start.4 = (f32[8,16,1,6]{2,0,3,1:T(8,128)S(1)}, f32[8,16,1,6]{2,0,3,1:T(8,128)}, u32[]{:S(2)}, u32[]{:S(2)}) collective-permute-start(f32[8,16,1,6]{2,0,3,1:T(8,128)S(1)} %get-tuple-element.27), channel_id=1, source_target_pairs={{0,3},{1,4},{2,5},{3,6},{4,7},{5,0},{6,1},{7,2},{8,11},{9,12},{10,... | collective-permute-start | bytes 9224 | tf_op jit(solution)/shard_map/ppermute | solution.py:65
  80.1 66.5 %collective-permute-start.5 = (f32[8,16,1,6]{2,0,3,1:T(8,128)S(1)}, f32[8,16,1,6]{2,0,3,1:T(8,128)S(1)}, u32[]{:S(2)}, u32[]{:S(2)}) collective-permute-start(f32[8,16,1,6]{2,0,3,1:T(8,128)S(1)} %get-tuple-element.26), channel_id=1, source_target_pairs={{0,2},{1,3},{2,4},{3,5},{4,6},{5,7},{6,0},{7,1},{8,10},{9,11},{10,... | collective-permute-start | bytes 9224 | tf_op jit(solution)/shard_map/ppermute | solution.py:65
  91.8 55.5 %collective-permute-start.6 = (f32[8,16,1,6]{2,0,3,1:T(8,128)S(1)}, f32[8,16,1,6]{2,0,3,1:T(8,128)S(1)}, u32[]{:S(2)}, u32[]{:S(2)}) collective-permute-start(f32[8,16,1,6]{2,0,3,1:T(8,128)S(1)} %get-tuple-element.25), channel_id=1, source_target_pairs={{0,1},{1,2},{2,3},{3,4},{4,5},{5,6},{6,7},{7,0},{8,9},{9,10},{10,1... | collective-permute-start | bytes 9224 | tf_op jit(solution)/shard_map/ppermute | solution.py:65
